TPU v7x, 256 devices: a whole 4x4x8 slice. The times are simulated.
256 devices in a mesh: row: 32 (over z, x_hi, core), col: 8 (over x_lo, y).
Axes of the slice: x: 4 (x_hi: 2, x_lo: 2; x = x_hi * 2 + x_lo), y: 4, z: 8, core: 2. Of those that a mesh axis runs over, the one named last changes fastest.
Arguments:
- tokens: bfloat16 [2048, 12288], P('col', 'row'), may hold values from -6 to 6
- weight: bfloat16 [12288, 24576], P('row', 'col'), may hold values from -0.0546875 to 0.0546875
- pre_act: bfloat16 [2048, 24576], P('row', 'col'), may hold values from -6 to 6
- out_grad: bfloat16 [2048, 24576], P('row', 'col'), may hold values from -6 to 6
Outputs:
- input_grad: bfloat16 [2048, 12288], P('col', 'row')
- weight_grad: bfloat16 [12288, 24576], P('row', 'col')
- left_stats: bfloat16 [12288, 24576], P('row', 'col')
- right_stats: bfloat16 [12288, 24576], P('row', 'col')
All inputs are finite; a program needn't handle non-finite values.
Results may differ from a plain program's by a relative error of at most 0.0054.
Values may be sent and summed in bfloat16 or wider, within the bound.
A program may use at most 128 MiB of HBM per device.

v0:
```python
import math
import jax
import jax.numpy as jnp
from jax import lax
from jax.sharding import PartitionSpec as P

BLOCK = 384


def gelu_slope(value):
    coeff = math.sqrt(2.0 / math.pi)
    inner = coeff * (value + 0.044715 * value * value * value)
    tanh_u = jnp.tanh(inner)
    return 0.5 * (1.0 + tanh_u) + 0.5 * value * (1.0 - tanh_u * tanh_u) * coeff * (
        1.0 + 3.0 * 0.044715 * value * value
    )


def on_device(tokens, weight, pre_act, out_grad):
    x_all = lax.all_gather(tokens, "col", axis=0, tiled=True)
    num_tokens = x_all.shape[0]
    rows_here = weight.shape[0]
    cols_here = weight.shape[1]
    hidden_grad = (out_grad.astype(jnp.float32) * gelu_slope(pre_act.astype(jnp.float32))).astype(
        jnp.bfloat16
    )
    grad_all = lax.all_gather(hidden_grad, "row", axis=0, tiled=True)
    partial_value = lax.dot_general(
        grad_all, weight, (((1,), (1,)), ((), ())), preferred_element_type=jnp.float32
    )
    weight_sum = lax.dot_general(
        x_all, grad_all, (((0,), (0,)), ((), ())), preferred_element_type=jnp.float32
    )
    input_grad = lax.psum_scatter(partial_value, "col", scatter_dimension=0, tiled=True).astype(
        jnp.bfloat16
    )
    scale = 1.0 / (BLOCK * num_tokens)
    tiles = weight_sum.reshape(rows_here // BLOCK, BLOCK, cols_here // BLOCK, BLOCK)
    left = jnp.einsum("ipjq,irjq->ipjr", tiles, tiles, precision=lax.Precision.HIGHEST) * scale
    right = jnp.einsum("ipjq,ipjr->iqjr", tiles, tiles, precision=lax.Precision.HIGHEST) * scale
    left_stats = left.reshape(rows_here, cols_here).astype(jnp.bfloat16)
    right_stats = right.reshape(rows_here, cols_here).astype(jnp.bfloat16)
    return (input_grad, weight_sum.astype(jnp.bfloat16), left_stats, right_stats)


def solution(mesh):
    in_specs = (P("col", "row"), P("row", "col"), P("row", "col"), P("row", "col"))
    out_specs = (P("col", "row"), P("row", "col"), P("row", "col"), P("row", "col"))
    return jax.shard_map(
        on_device, mesh=mesh, in_specs=in_specs, out_specs=out_specs, check_vma=False
    )
```

profile of v0, /device:TPU:4, one launch (start us, length us, event | category | flops | bytes accessed | tf_op | source)
XLA Modules:
  0.0 233.7 jit_solution(4617175206382753291)
XLA Ops:
  7.2 0.0 copy-start
  7.2 0.0 all-gather.3.cloned.1.call-start
  7.2 2.6 %fusion.7 = bf16[64,3072]{1,0:T(8,128)(2,1)} fusion(bf16[64,3072]{1,0:T(8,128)(2,1)} %param.6, bf16[64,3072]{1,0:T(8,128)(2,1)} %param.7), kind=kLoop, calls=%fused_computation.17 | loop fusion | flops 4128768 | bytes 1179648 | tf_op jit(solution)/shard_map/convert_element_type | solution.py:24
  9.8 0.0 all-gather.3.cloned.1.call-update
  9.8 0.0 all-gather.5.cloned.1.call-start
  9.9 0.7 all-gather.5.cloned.1.call-update
  10.6 0.0 reduce-scatter.2.cloned.1.call-start
  10.6 118.4 %all-gather.3.cloned.1.call-done = bf16[2048,3072]{1,0:T(8,128)(2,1)} async-done(((bf16[64,3072]{1,0:T(8,128)(2,1)}), bf16[2048,3072]{1,0:T(8,128)(2,1)}) %all-gather.3.cloned.1.call-update) | async-done | bytes 12582928 | tf_op jit(solution)/shard_map/all_gather | solution.py:27
  129.0 0.0 copy-done
  129.0 10.8 %fusion.9 = f32[2048,384]{1,0:T(8,128)} fusion(bf16[2048,3072]{1,0:T(8,128)(2,1)} %all-gather.3.cloned.1.call-done, bf16[384,3072]{1,0:T(8,128)(2,1)S(1)} %copy-done), kind=kOutput, calls=%fused_computation.19 | convolution fusion | flops 4831838208 | bytes 18087936 | tf_op jit(solution)/shard_map/dot_general | solution.py:28
  139.8 0.0 reduce-scatter.2.cloned.1.call-update
  139.8 32.6 %all-gather.5.cloned.1.call-done = bf16[2048,384]{1,0:T(8,128)(2,1)} async-done(((bf16[256,384]{1,0:T(8,128)(2,1)}), bf16[2048,384]{1,0:T(8,128)(2,1)}) %all-gather.5.cloned.1.call-update) | async-done | bytes 1572880 | tf_op jit(solution)/shard_map/all_gather | solution.py:20
  172.4 12.1 %bitcast_convert_fusion = (bf16[384,3072]{0,1:T(8,128)(2,1)}, f32[3072,384]{1,0:T(8,128)}) fusion(bf16[2048,3072]{1,0:T(8,128)(2,1)} %all-gather.3.cloned.1.call-done, bf16[2048,384]{1,0:T(8,128)(2,1)} %all-gather.5.cloned.1.call-done), kind=kOutput, calls=%fused_computation | convolution fusion | flops 4833017856 | bytes 21233664 | tf_op jit(solution)/shard_map/dot_general | solution.py:31
  184.5 4.3 %copy.11 = bf16[384,3072]{1,0:T(8,128)(2,1)} copy(bf16[384,3072]{0,1:T(8,128)(2,1)} %get-tuple-element.8) | data formatting | bytes 4718592
  188.7 14.0 %multiply_convert_fusion.1 = bf16[8,384,384]{2,1,0:T(8,128)(2,1)} fusion(f32[384,8,384]{0,2,1:T(8,128)} %bitcast.22), kind=kOutput, calls=%fused_computation.2 | convolution fusion | flops 5438177280 | bytes 7077888 | tf_op jit(solution)/shard_map/ipjq,irjq->ipjr/dot_general | solution.py:39
  202.8 4.3 %copy.12 = bf16[384,3072]{1,0:T(8,128)(2,1)} copy(bf16[384,3072]{0,1:T(8,128)(2,1)} %bitcast.25) | data formatting | bytes 4718592
  207.0 14.2 %multiply_convert_fusion = bf16[8,384,384]{2,1,0:T(8,128)(2,1)} fusion(f32[384,8,384]{0,2,1:T(8,128)} %bitcast.23), kind=kOutput, calls=%fused_computation.1 | convolution fusion | flops 5438177280 | bytes 7077888 | tf_op jit(solution)/shard_map/ipjq,ipjr->iqjr/dot_general | solution.py:40
  221.2 4.3 %copy.13 = bf16[384,3072]{1,0:T(8,128)(2,1)} copy(bf16[384,3072]{0,1:T(8,128)(2,1)} %bitcast.24) | data formatting | bytes 4718592
  225.5 0.0 reduce-scatter.2.cloned.1.call-done
  225.5 1.7 convert_element_type.42
Async XLA Ops:
  7.2 121.8 %copy-start = (bf16[384,3072]{1,0:T(8,128)(2,1)S(1)}, bf16[384,3072]{1,0:T(8,128)(2,1)}, u32[]{:S(2)}) copy-start(bf16[384,3072]{1,0:T(8,128)(2,1)} %param.5) | copy-start | bytes 7077892
  7.2 121.8 %all-gather.3.cloned.1.call-start = ((), (), s32[]{:S(2)}) async-start(), calls=%async_computation.1 | async-start | bytes 12976128 | tf_op jit(solution)/shard_map/all_gather | solution.py:27
  9.8 162.6 %all-gather.5.cloned.1.call-start = ((), (), s32[]{:S(2)}) async-start(), calls=%async_computation.3 | async-start | bytes 1769472 | tf_op jit(solution)/shard_map/all_gather | solution.py:20
  10.6 215.0 %reduce-scatter.2.cloned.1.call-start = ((), (), s32[]{:S(2)}) async-start(), calls=%async_computation.2 | async-start | bytes 3538944 | tf_op jit(solution)/shard_map/reduce_scatter | solution.py:34
Sparse Core Ops, SparseCore 0:
  11.3 117.6 all-gather.2
  130.8 41.5 all-gather.4
  175.0 48.3 reduce-scatter.1
where the time goes:
time: 234 us
  waiting for transfers between devices  152 us (65%)
  matrix products  51.1 us (22%)
  between operations  13.8 us (6%)
  local copies, waits for them, and re-layouts  12.8 us (5%)
  other arithmetic  4.26 us (2%)
    all_gather x1, waiting for transfers between devices, on_device(): grad_all = lax.all_gather(hidden_grad, 'row', axis=0, tiled=True)  118 us
    all_gather x1, waiting for transfers between devices, on_device(): x_all = lax.all_gather(tokens, 'col', axis=0, tiled=True)  32.6 us
    dot_general x1, matrix products, on_device(): jnp.einsum('ipjq,ipjr->iqjr', tiles, tiles, precision=lax.Precision.HIGHEST)  14.2 us
    dot_general x1, matrix products, on_device(): jnp.einsum('ipjq,irjq->ipjr', tiles, tiles, precision=lax.Precision.HIGHEST)  14 us
    unnamed x5, local copies, waits for them, and re-layouts  12.8 us
    dot_general x1, matrix products, on_device(): lax.dot_general(x_all, grad_all, (((0,), (0,)), ((), ())), preferred_elem...  12.1 us
    dot_general x1, matrix products, on_device(): lax.dot_general(grad_all, weight, (((1,), (1,)), ((), ())), preferred_ele...  10.8 us
  transfers between devices with their start and end apart: 3, of which 2 were waited for; matrix products, arithmetic and copies ran while one was open for 27% of the time, Pallas kernels for 0%

commit v1 on v0

--- a/solution.py
+++ b/solution.py
@@ -24,7 +24,9 @@
     hidden_grad = (out_grad.astype(jnp.float32) * gelu_slope(pre_act.astype(jnp.float32))).astype(
         jnp.bfloat16
     )
-    grad_all = lax.all_gather(hidden_grad, "row", axis=0, tiled=True)
+    grad_all = jnp.concatenate(
+        lax.all_to_all(jnp.stack([hidden_grad] * lax.axis_size("row")), "row", 0, 0), axis=0
+    )
     partial_value = lax.dot_general(
         grad_all, weight, (((1,), (1,)), ((), ())), preferred_element_type=jnp.float32
     )

time: 234 us -> 371 us (1.59)
  waiting for transfers between devices: 152 us -> 275 us
  starting transfers between devices: 0.12 us -> 11.7 us
  local copies, waits for them, and re-layouts: 12.8 us -> 18.9 us
  matrix products: 51.1 us -> 47.3 us
    all_to_all x0 -> x1, waiting for transfers between devices: none -> 274 us  [on_device(): lax.all_to_all(jnp.stack([hidden_grad] * lax.axis_size('row')), 'row', 0, 0)]
    all_gather x1 -> x0, waiting for transfers between devices: 118 us -> none  [on_device(): grad_all = lax.all_gather(hidden_grad, 'row', axis=0, tiled=True)]
    all_gather x1, waiting for transfers between devices: 32.6 us -> 0.02 us  [on_device(): x_all = lax.all_gather(tokens, 'col', axis=0, tiled=True)]
    all_to_all x0 -> x1, starting transfers between devices: none -> 11.6 us  [on_device(): lax.all_to_all(jnp.stack([hidden_grad] * lax.axis_size('row')), 'row', 0, 0)]
    another operation x0 -> x1, local copies, waits for them, and re-layouts: none -> 6.08 us  [on_device(): jnp.stack([hidden_grad] * lax.axis_size('row'))]
    unnamed x5 -> x7, local copies, waits for them, and re-layouts: 12.8 us -> 12.8 us
  transfers between devices with their start and end apart: 3 -> 3, of which waited for: 2 -> 1; matrix products, arithmetic and copies ran while one was open for 27% -> 16% of each run, Pallas kernels for 0% -> 0%
where the time goes in v1:
time: 371 us; the launch traced here: 370 us
  waiting for transfers between devices  275 us (74%)
  matrix products  47.3 us (13%)
  local copies, waits for them, and re-layouts  18.9 us (5%)
  between operations  14.1 us (4%)
  starting transfers between devices  11.7 us (3%)
    all_to_all x1, waiting for transfers between devices, on_device(): lax.all_to_all(jnp.stack([hidden_grad] * lax.axis_size('row')), 'row', 0, 0)  274 us
    dot_general x1, matrix products, on_device(): jnp.einsum('ipjq,ipjr->iqjr', tiles, tiles, precision=lax.Precision.HIGHEST)  14 us
    unnamed x7, local copies, waits for them, and re-layouts  12.8 us
    all_to_all x1, starting transfers between devices, on_device(): lax.all_to_all(jnp.stack([hidden_grad] * lax.axis_size('row')), 'row', 0, 0)  11.6 us
    dot_general x1, matrix products, on_device(): lax.dot_general(x_all, grad_all, (((0,), (0,)), ((), ())), preferred_elem...  11.3 us
    dot_general x1, matrix products, on_device(): jnp.einsum('ipjq,irjq->ipjr', tiles, tiles, precision=lax.Precision.HIGHEST)  11.2 us
    dot_general x1, matrix products, on_device(): lax.dot_general(grad_all, weight, (((1,), (1,)), ((), ())), preferred_ele...  10.8 us
  transfers between devices with their start and end apart: 3, of which 1 were waited for; matrix products, arithmetic and copies ran while one was open for 16% of the time, Pallas kernels for 0%

profile of v1, /device:TPU:4, one launch (start us, length us, event | category | flops | bytes accessed | tf_op | source)
XLA Modules:
  0.0 370.4 jit_solution(9259590298631019683)
XLA Ops:
  7.2 0.0 copy-start
  7.2 1.8 fusion.7
  9.0 6.1 %stack.2 = bf16[32,64,3072]{2,1,0:T(8,128)(2,1)} broadcast(bf16[64,3072]{1,0:T(8,128)(2,1)S(1)} %fusion.7), dimensions={1,2} | broadcast | bytes 12976128 | tf_op jit(solution)/shard_map/stack | solution.py:28
  15.1 11.6 %all-to-all-start = ((bf16[32,64,3072]{2,1,0:T(8,128)(2,1)}), bf16[32,64,3072]{2,1,0:T(8,128)(2,1)}, u32[]{:S(2)}, u32[]{:S(2)}) async-start(bf16[32,64,3072]{2,1,0:T(8,128)(2,1)} %stack.2), calls=%async_computation | async-start | bytes 25165824 | tf_op jit(solution)/shard_map/all_to_all | solution.py:28
  26.7 0.0 all-gather.2.cloned.1.call-start
  26.8 0.7 all-gather.2.cloned.1.call-update
  27.5 0.0 reduce-scatter.2.cloned.1.call-start
  27.5 274.2 %all-to-all-done = bf16[32,64,3072]{2,1,0:T(8,128)(2,1)} async-done(((bf16[32,64,3072]{2,1,0:T(8,128)(2,1)}), bf16[32,64,3072]{2,1,0:T(8,128)(2,1)}, u32[]{:S(2)}, u32[]{:S(2)}) %all-to-all-start) | async-done | bytes 12582944 | tf_op jit(solution)/shard_map/all_to_all | solution.py:28
  301.7 0.0 copy-done
  301.7 10.8 %fusion.9 = f32[2048,384]{1,0:T(8,128)} fusion(bf16[2048,3072]{1,0:T(8,128)(2,1)} %bitcast, bf16[384,3072]{1,0:T(8,128)(2,1)S(1)} %copy-done), kind=kOutput, calls=%fused_computation.19 | convolution fusion | flops 4831838208 | bytes 18087936 | tf_op jit(solution)/shard_map/dot_general | solution.py:30
  312.5 0.0 reduce-scatter.2.cloned.1.call-update
  312.5 0.0 all-gather.2.cloned.1.call-done
  312.5 11.3 %bitcast_convert_fusion = (bf16[384,3072]{0,1:T(8,128)(2,1)}, f32[3072,384]{1,0:T(8,128)S(1)}) fusion(bf16[2048,3072]{1,0:T(8,128)(2,1)} %bitcast, bf16[2048,384]{1,0:T(8,128)(2,1)} %all-gather.2.cloned.1.call-done), kind=kOutput, calls=%fused_computation | convolution fusion | flops 4833017856 | bytes 21233664 | tf_op jit(solution)/shard_map/dot_general | solution.py:33
  323.8 0.0 copy-start.1
  323.8 11.2 %multiply_convert_fusion.1 = bf16[8,384,384]{2,1,0:T(8,128)(2,1)} fusion(f32[384,8,384]{0,2,1:T(8,128)S(1)} %bitcast.23), kind=kOutput, calls=%fused_computation.2 | convolution fusion | flops 5438177280 | bytes 7077888 | tf_op jit(solution)/shard_map/ipjq,irjq->ipjr/dot_general | solution.py:41
  335.0 0.0 copy-done.1
  335.0 4.3 %copy.12 = bf16[384,3072]{1,0:T(8,128)(2,1)} copy(bf16[384,3072]{0,1:T(8,128)(2,1)} %bitcast.26) | data formatting | bytes 4718592
  339.3 14.0 %multiply_convert_fusion = bf16[8,384,384]{2,1,0:T(8,128)(2,1)} fusion(f32[384,8,384]{0,2,1:T(8,128)} %bitcast.24), kind=kOutput, calls=%fused_computation.1 | convolution fusion | flops 5438177280 | bytes 7077888 | tf_op jit(solution)/shard_map/ipjq,ipjr->iqjr/dot_general | solution.py:42
  353.3 4.3 %copy.13 = bf16[384,3072]{1,0:T(8,128)(2,1)} copy(bf16[384,3072]{0,1:T(8,128)(2,1)} %bitcast.25) | data formatting | bytes 4718592
  357.6 4.3 %copy.11 = bf16[384,3072]{1,0:T(8,128)(2,1)} copy(bf16[384,3072]{0,1:T(8,128)(2,1)} %get-tuple-element.8) | data formatting | bytes 4718592
  361.9 0.0 reduce-scatter.2.cloned.1.call-done
  361.9 1.7 convert_element_type.42
Async XLA Ops:
  7.2 294.5 %copy-start = (bf16[384,3072]{1,0:T(8,128)(2,1)S(1)}, bf16[384,3072]{1,0:T(8,128)(2,1)}, u32[]{:S(2)}) copy-start(bf16[384,3072]{1,0:T(8,128)(2,1)} %param.5) | copy-start | bytes 7077892
  15.1 286.6 %all-to-all-start = ((bf16[32,64,3072]{2,1,0:T(8,128)(2,1)}), bf16[32,64,3072]{2,1,0:T(8,128)(2,1)}, u32[]{:S(2)}, u32[]{:S(2)}) async-start(bf16[32,64,3072]{2,1,0:T(8,128)(2,1)} %stack.2), calls=%async_computation | async-start | bytes 25165824 | tf_op jit(solution)/shard_map/all_to_all | solution.py:28
  26.7 285.8 %all-gather.2.cloned.1.call-start = ((), (), s32[]{:S(2)}) async-start(), calls=%async_computation.3 | async-start | bytes 1769472 | tf_op jit(solution)/shard_map/all_gather | solution.py:20
  27.5 334.4 %reduce-scatter.2.cloned.1.call-start = ((), (), s32[]{:S(2)}) async-start(), calls=%async_computation.2 | async-start | bytes 3538944 | tf_op jit(solution)/shard_map/reduce_scatter | solution.py:36
  323.8 11.2 %copy-start.1 = (f32[3072,384]{1,0:T(8,128)}, f32[3072,384]{1,0:T(8,128)S(1)}, u32[]{:S(2)}) copy-start(f32[3072,384]{1,0:T(8,128)S(1)} %get-tuple-element.9) | copy-start | bytes 14155780
Sparse Core Ops, SparseCore 0:
  29.3 58.1 all-gather.1
  312.6 47.4 reduce-scatter.1
